TPU v7x, 512 devices: a whole 4x8x8 slice. The times are simulated.
512 devices in a mesh: seq: 32 (over y, x), trow: 2 (over core), tcol: 8 (over z).
Axes of the slice: x: 4, y: 8, z: 8, core: 2. Of those that a mesh axis runs over, the one named last changes fastest.
Arguments:
- tokens: bfloat16 [16384, 4096], P('seq', ('trow', 'tcol')), may hold values from -24 to 24
- norm_gain: float32 [4096], replicated, may hold values from 0.1 to 1.9
- in_weight: bfloat16 [3, 4096, 8192], P(None, None, ('trow', 'tcol')), may hold values from -0.09375 to 0.09375
- filter_taps: float32 [128, 8192], P(None, ('trow', 'tcol')), may hold values from -0.5 to 0.5
- conv_skip: float32 [8192], P(('trow', 'tcol')), may hold values from -1 to 1
- out_weight: bfloat16 [8192, 4096], P(('trow', 'tcol')), may hold values from -0.09375 to 0.09375
Outputs:
- mixer_out: bfloat16 [16384, 4096], P('seq', ('trow', 'tcol'))
All inputs are finite; a program needn't handle non-finite values.
Results may differ from a plain program's by a relative error of at most 0.03.
Values may be sent and summed in bfloat16 or wider, within the bound.
A program may use at most 64 MiB of HBM per device.

v0:
```python
import jax
import jax.numpy as jnp
from jax import lax
from jax.sharding import PartitionSpec as P


def passed_along(block, axis, distance):
    devices = range(lax.axis_size(axis))
    route = [(i - distance, i) for i in devices if i - distance in devices]
    return lax.ppermute(block, axis, route)


def on_device(tokens, norm_gain, in_weight, filter_taps, conv_skip, out_weight):
    whole = lax.all_gather(tokens, ("trow", "tcol"), axis=1, tiled=True)
    wide = whole.astype(jnp.float32)
    mean_square = jnp.mean(wide * wide, axis=1, keepdims=True)
    normed = (wide * lax.rsqrt(mean_square + 1e-06) * norm_gain).astype(jnp.bfloat16)
    query = jnp.dot(normed, in_weight[0], preferred_element_type=jnp.float32).astype(jnp.bfloat16)
    keys = jnp.dot(normed, in_weight[1], preferred_element_type=jnp.float32).astype(jnp.bfloat16)
    values = jnp.dot(normed, in_weight[2], preferred_element_type=jnp.float32).astype(jnp.bfloat16)
    mixed = (keys.astype(jnp.float32) * values.astype(jnp.float32)).astype(jnp.bfloat16)
    taps = filter_taps.shape[0]
    rows = mixed.shape[0]
    channels = mixed.shape[1]
    tail_rows = mixed[rows - (taps - 1) :]
    previous = passed_along(tail_rows, "seq", 1)
    extended = jnp.concatenate([previous, mixed], axis=0)

    def tap_group(group, total):
        for inner in range(8):
            index = group * 8 + inner
            window = lax.dynamic_slice_in_dim(extended, taps - 1 - index, rows, 0)
            weight = lax.dynamic_slice_in_dim(filter_taps, index, 1, 0)
            total = total + window.astype(jnp.float32) * weight
        return total

    filtered = lax.fori_loop(0, taps // 8, tap_group, jnp.zeros((rows, channels), jnp.float32))
    filtered = filtered + conv_skip * mixed.astype(jnp.float32)
    gated = (query.astype(jnp.float32) * filtered).astype(jnp.bfloat16)
    partial_sum = jnp.dot(gated, out_weight, preferred_element_type=jnp.float32)
    summed = lax.psum_scatter(
        partial_sum.astype(jnp.bfloat16), ("trow", "tcol"), scatter_dimension=1, tiled=True
    )
    return summed


def solution(mesh):
    placed = (
        P("seq", ("trow", "tcol")),
        P(),
        P(None, None, ("trow", "tcol")),
        P(None, ("trow", "tcol")),
        P(("trow", "tcol")),
        P(("trow", "tcol"), None),
    )
    return jax.shard_map(
        on_device, mesh=mesh, in_specs=placed, out_specs=P("seq", ("trow", "tcol")), check_vma=False
    )
```

profile of v0, /device:TPU:1, one launch (start us, length us, event | category | flops | bytes accessed | tf_op | source)
XLA Modules:
  0.0 220.7 jit_solution(7478278523960679927)
XLA Ops:
  6.5 0.0 all-gather.2.cloned.1.call-start
  6.5 0.7 all-gather.2.cloned.1.call-update
  7.3 0.0 reduce-scatter.2.cloned.1.call-start
  7.3 59.9 %all-gather.2.cloned.1.call-done = bf16[512,4096]{1,0:T(8,128)(2,1)} async-done(((bf16[512,256]{1,0:T(8,128)(2,1)}), bf16[512,4096]{1,0:T(8,128)(2,1)}) %all-gather.2.cloned.1.call-update) | async-done | bytes 4194320 | tf_op jit(solution)/shard_map/all_gather | solution.py:14
  67.2 3.2 %fusion.7 = f32[512]{0:T(512)S(1)} fusion(bf16[512,4096]{1,0:T(8,128)(2,1)} %all-gather.2.cloned.1.call-done), kind=kLoop, calls=%fused_computation.18 | loop fusion | flops 6290944 | bytes 4196352 | tf_op jit(solution)/shard_map/reduce_sum | solution.py:16
  70.4 0.2 copy-done
  70.6 4.6 %fusion.46 = f32[512,512]{1,0:T(8,128)S(1)} fusion(bf16[3,4096,512]{2,1,0:T(8,128)(2,1)} %param.10, bf16[512,4096]{1,0:T(8,128)(2,1)S(1)} %copy-done, f32[4096]{0:T(1024)S(1)} %copy-done.1, f32[512]{0:T(512)S(1)} %add_rsqrt_fusion), kind=kOutput, calls=%fused_computation.40 | convolution fusion | flops 2156396544 | bytes 9455616 | tf_op jit(solution)/shard_map/dot_general | solution.py:20
  75.2 4.6 %fusion.40 = bf16[512,512]{1,0:T(8,128)(2,1)S(1)} fusion(f32[512,512]{1,0:T(8,128)S(1)} %fusion.46, bf16[3,4096,512]{2,1,0:T(8,128)(2,1)} %param.10, bf16[512,4096]{1,0:T(8,128)(2,1)S(1)} %copy-done, f32[4096]{0:T(1024)S(1)} %copy-done.1, f32[512]{0:T(512)S(1)} %add_rsqrt_fusion), kind=kOutput, calls=%fused_computation.38 | convolution fusion | flops 2156920832 | bytes 9979904 | tf_op jit(solution)/shard_map/dot_general | solution.py:19
  79.8 3.1 %collective-permute-start = (bf16[127,512]{1,0:T(8,128)(2,1)S(1)}, bf16[127,512]{1,0:T(8,128)(2,1)S(1)}, u32[]{:S(2)}, u32[]{:S(2)}) collective-permute-start(bf16[127,512]{1,0:T(8,128)(2,1)S(1)} %slice.16), channel_id=1, source_target_pairs={{0,16},{16,32},{32,48},{48,64},{64,80},{80,96},{96,112},{112,128},... | collective-permute-start | bytes 390152 | tf_op jit(solution)/shard_map/ppermute | solution.py:10
  82.9 2.6 %collective-permute-done = bf16[127,512]{1,0:T(8,128)(2,1)S(1)} collective-permute-done((bf16[127,512]{1,0:T(8,128)(2,1)S(1)}, bf16[127,512]{1,0:T(8,128)(2,1)S(1)}, u32[]{:S(2)}, u32[]{:S(2)}) %collective-permute-start) | collective-permute-done | bytes 130080 | tf_op jit(solution)/shard_map/ppermute | solution.py:10
  85.5 0.1 pad_maximum_fusion
  85.6 0.0 copy-start.2
  85.6 39.9 %while.17 = (s32[]{:T(128)}, f32[512,512]{1,0:T(8,128)S(1)}, bf16[639,512]{1,0:T(8,128)(2,1)S(1)}, f32[128,512]{1,0:T(8,128)}, s32[]{:T(128)}, /*index=5*/s32[]{...) while((s32[]{:T(128)}, f32[512,512]{1,0:T(8,128)S(1)}, ...), condition=%wide.region_2.0_spmd.clone, body=%wide.region_1.0_spmd.clone.sunk | while | flops 6553667 | bytes 6341631 | solution.py:37
  85.7 1.0 constant_dynamic-slice_fusion.9
  86.8 1.4 fusion.58
  88.2 1.0 constant_dynamic-slice_fusion.9
  89.3 1.3 fusion.58
  90.7 1.0 constant_dynamic-slice_fusion.9
  91.8 1.4 fusion.58
  93.2 1.0 constant_dynamic-slice_fusion.9
  94.3 1.3 fusion.58
  95.7 1.0 constant_dynamic-slice_fusion.9
  96.8 1.4 fusion.58
  98.2 1.0 constant_dynamic-slice_fusion.9
  99.2 1.3 fusion.58
  100.7 1.0 constant_dynamic-slice_fusion.9
  101.7 1.4 fusion.58
  103.2 1.0 constant_dynamic-slice_fusion.9
  104.2 1.3 fusion.58
  105.7 1.0 constant_dynamic-slice_fusion.9
  106.7 1.4 fusion.58
  108.2 1.0 constant_dynamic-slice_fusion.9
  109.2 1.3 fusion.58
  110.7 1.0 constant_dynamic-slice_fusion.9
  111.7 1.4 fusion.58
  113.2 1.0 constant_dynamic-slice_fusion.9
  114.2 1.3 fusion.58
  115.7 1.0 constant_dynamic-slice_fusion.9
  116.7 1.4 fusion.58
  118.1 1.0 constant_dynamic-slice_fusion.9
  119.2 1.3 fusion.58
  120.6 1.0 constant_dynamic-slice_fusion.9
  121.7 1.4 fusion.58
  123.1 1.0 constant_dynamic-slice_fusion.9
  124.2 1.3 fusion.58
  125.5 11.2 %convolution_convert_fusion = bf16[512,4096]{1,0:T(8,128)(2,1)} fusion(bf16[512,4096]{1,0:T(8,128)(2,1)} %param.13, bf16[3,4096,512]{2,1,0:T(8,128)(2,1)} %param.10, f32[512,512]{1,0:T(8,128)S(1)} %get-tuple-element.156, bf16[512,512]{1,0:T(8,128)(2,1)S(1)} %fusion.40, f32[512]{0:T(512)S(1)} %copy-done.2, ...), kind=kOutput, calls=%fused_computation.21 | convolution fusion | flops 4307288064 | bytes 18370560 | tf_op jit(solution)/shard_map/dot_general | solution.py:40
  136.8 0.0 reduce-scatter.2.cloned.1.call-update
  136.8 77.0 %reduce-scatter.2.cloned.1.call-done = bf16[512,256]{1,0:T(8,128)(2,1)} async-done(((bf16[512,4096]{1,0:T(8,128)(2,1)}), bf16[512,256]{1,0:T(8,128)(2,1)}) %reduce-scatter.2.cloned.1.call-update) | async-done | bytes 262160 | tf_op jit(solution)/shard_map/reduce_scatter | solution.py:41
  (7 shorter events, 0.1 us)
Async XLA Ops:
  6.5 63.9 %copy-start.1 = (f32[4096]{0:T(1024)S(1)}, f32[4096]{0:T(1024)}, u32[]{:S(2)}) copy-start(f32[4096]{0:T(1024)} %param.9) | copy-start | bytes 49156
  6.5 60.6 %all-gather.2.cloned.1.call-start = ((), (), s32[]{:S(2)}) async-start(), calls=%async_computation.1 | async-start | bytes 4456448 | tf_op jit(solution)/shard_map/all_gather | solution.py:14
  7.3 206.6 %reduce-scatter.2.cloned.1.call-start = ((), (), s32[]{:S(2)}) async-start(), calls=%async_computation.2 | async-start | bytes 4456448 | tf_op jit(solution)/shard_map/reduce_scatter | solution.py:41
  67.2 3.4 %copy-start = (bf16[512,4096]{1,0:T(8,128)(2,1)S(1)}, bf16[512,4096]{1,0:T(8,128)(2,1)}, u32[]{:S(2)}) copy-start(bf16[512,4096]{1,0:T(8,128)(2,1)} %all-gather.2.cloned.1.call-done) | copy-start | bytes 12582916
  79.8 5.7 %collective-permute-start = (bf16[127,512]{1,0:T(8,128)(2,1)S(1)}, bf16[127,512]{1,0:T(8,128)(2,1)S(1)}, u32[]{:S(2)}, u32[]{:S(2)}) collective-permute-start(bf16[127,512]{1,0:T(8,128)(2,1)S(1)} %slice.16), channel_id=1, source_target_pairs={{0,16},{16,32},{32,48},{48,64},{64,80},{80,96},{96,112},{112,128},... | collective-permute-start | bytes 390152 | tf_op jit(solution)/shard_map/ppermute | solution.py:10
  85.6 39.9 %copy-start.2 = (f32[512]{0:T(512)S(1)}, f32[512]{0:T(512)}, u32[]{:S(2)}) copy-start(f32[512]{0:T(512)} %param.12) | copy-start | bytes 6148
Sparse Core Ops, SparseCore 0:
  9.4 57.7 all-gather.1
  136.9 76.8 reduce-scatter.1
where the time goes:
time: 222 us; the launch traced here: 221 us
  waiting for transfers between devices  140 us (63%)
  other arithmetic  25 us (11%)
  matrix products  20.4 us (9%)
  local copies, waits for them, and re-layouts  16.9 us (8%)
  between operations  13.5 us (6%)
  starting transfers between devices  3.13 us (1%)
    reduce_scatter x1, waiting for transfers between devices, on_device(): lax.psum_scatter(partial_sum.astype(jnp.bfloat16), ('trow', 'tcol'), scat...  77 us
    all_gather x1, waiting for transfers between devices, on_device(): whole = lax.all_gather(tokens, ('trow', 'tcol'), axis=1, tiled=True)  59.9 us
    add x16, other arithmetic, tap_group(): total = total + window.astype(jnp.float32) * weight  21.6 us
    dynamic_slice x16, local copies, waits for them, and re-layouts, tap_group(): weight = lax.dynamic_slice_in_dim(filter_taps, index, 1, 0)  16.6 us
    dot_general x1, matrix products, on_device(): partial_sum = jnp.dot(gated, out_weight, preferred_element_type=jnp.float32)  11.2 us
    dot_general x1, matrix products, on_device(): jnp.dot(normed, in_weight[1], preferred_element_type=jnp.float32)  4.58 us
    dot_general x1, matrix products, on_device(): jnp.dot(normed, in_weight[2], preferred_element_type=jnp.float32)  4.56 us
  transfers between devices with their start and end apart: 3, of which 3 were waited for; matrix products, arithmetic and copies ran while one was open for 0% of the time, Pallas kernels for 0%

commit v1 on v0

--- a/solution.py
+++ b/solution.py
@@ -1,7 +1,21 @@
+import functools
 import jax
 import jax.numpy as jnp
 from jax import lax
 from jax.sharding import PartitionSpec as P
+from jax.lax import all_to_all, axis_size
+
+
+def _wrap_screen(arr, across):
+    return jnp.concatenate(
+        all_to_all(
+            jnp.stack(axis_size(across) * [arr], 0), axis_name=across, split_axis=0, concat_axis=0
+        ),
+        1,
+    )
+
+
+recast_ratios = functools.partial(_wrap_screen, across=("trow", "tcol"))
 
 
 def passed_along(block, axis, distance):
@@ -11,7 +25,7 @@
 
 
 def on_device(tokens, norm_gain, in_weight, filter_taps, conv_skip, out_weight):
-    whole = lax.all_gather(tokens, ("trow", "tcol"), axis=1, tiled=True)
+    whole = recast_ratios(tokens)
     wide = whole.astype(jnp.float32)
     mean_square = jnp.mean(wide * wide, axis=1, keepdims=True)
     normed = (wide * lax.rsqrt(mean_square + 1e-06) * norm_gain).astype(jnp.bfloat16)

time: 222 us -> 275 us (1.24)
  waiting for transfers between devices: 140 us -> 173 us
  starting transfers between devices: 3.13 us -> 15.1 us
  local copies, waits for them, and re-layouts: 16.9 us -> 20.2 us
    all_to_all x0 -> x1, waiting for transfers between devices: none -> 92.9 us  [_wrap_screen(): all_to_all(jnp.stack(axis_size(across) * [arr], 0), axis_name=across, spl...]
    all_gather x1 -> x0, waiting for transfers between devices: 59.9 us -> none  [on_device(): whole = lax.all_gather(tokens, ('trow', 'tcol'), axis=1, tiled=True)]
    all_to_all x0 -> x1, starting transfers between devices: none -> 12 us  [_wrap_screen(): all_to_all(jnp.stack(axis_size(across) * [arr], 0), axis_name=across, spl...]
    convert_element_type x0 -> x1, other arithmetic: none -> 2.77 us  [on_device(): (wide * lax.rsqrt(mean_square + 1e-06) * norm_gain).astype(jnp.bfloat16)]
where the time goes in v1:
time: 275 us; the launch traced here: 273 us
  waiting for transfers between devices  173 us (63%)
  other arithmetic  27.6 us (10%)
  matrix products  21.8 us (8%)
  local copies, waits for them, and re-layouts  20.2 us (7%)
  starting transfers between devices  15.1 us (5%)
  between operations  13.5 us (5%)
    all_to_all x1, waiting for transfers between devices, _wrap_screen(): all_to_all(jnp.stack(axis_size(across) * [arr], 0), axis_name=across, spl...  92.9 us
    reduce_scatter x1, waiting for transfers between devices, on_device(): lax.psum_scatter(partial_sum.astype(jnp.bfloat16), ('trow', 'tcol'), scat...  77.6 us
    add x16, other arithmetic, tap_group(): total = total + window.astype(jnp.float32) * weight  21.6 us
    dynamic_slice x16, local copies, waits for them, and re-layouts, tap_group(): weight = lax.dynamic_slice_in_dim(filter_taps, index, 1, 0)  16.6 us
    all_to_all x1, starting transfers between devices, _wrap_screen(): all_to_all(jnp.stack(axis_size(across) * [arr], 0), axis_name=across, spl...  12 us
    dot_general x1, matrix products, on_device(): partial_sum = jnp.dot(gated, out_weight, preferred_element_type=jnp.float32)  11.2 us
    dot_general x1, matrix products, on_device(): jnp.dot(normed, in_weight[2], preferred_element_type=jnp.float32)  6.05 us
  transfers between devices with their start and end apart: 3, of which 3 were waited for; matrix products, arithmetic and copies ran while one was open for 0% of the time, Pallas kernels for 0%

profile of v1, /device:TPU:1, one launch (start us, length us, event | category | flops | bytes accessed | tf_op | source)
XLA Modules:
  0.0 272.9 jit_solution(6088613121360569682)
XLA Ops:
  6.5 1.1 copy.7
  7.6 2.4 stack.2
  10.0 12.0 %all-to-all-start = ((bf16[16,512,256]{1,2,0:T(8,128)(2,1)}), bf16[16,512,256]{1,2,0:T(8,128)(2,1)}, u32[]{:S(2)}, u32[]{:S(2)}) async-start(bf16[16,512,256]{1,2,0:T(8,128)(2,1)} %stack.2), calls=%async_computation | async-start | bytes 8388608 | tf_op jit(solution)/shard_map/all_to_all | solution.py:11
  22.0 0.0 reduce-scatter.2.cloned.1.call-start
  22.1 92.9 %all-to-all-done = bf16[16,512,256]{1,2,0:T(8,128)(2,1)} async-done(((bf16[16,512,256]{1,2,0:T(8,128)(2,1)}), bf16[16,512,256]{1,2,0:T(8,128)(2,1)}, u32[]{:S(2)}, u32[]{:S(2)}) %all-to-all-start) | async-done | bytes 4194336 | tf_op jit(solution)/shard_map/all_to_all | solution.py:11
  115.0 3.1 %fusion.7 = f32[512]{0:T(512)S(1)} fusion(bf16[16,512,256]{1,2,0:T(8,128)(2,1)} %all-to-all-done), kind=kLoop, calls=%fused_computation.18 | loop fusion | flops 6290944 | bytes 4196352 | tf_op jit(solution)/shard_map/reduce_sum | solution.py:30
  118.1 2.8 %fusion.9 = bf16[16,512,256]{1,2,0:T(8,128)(2,1)S(1)} fusion(bf16[16,512,256]{1,2,0:T(8,128)(2,1)} %all-to-all-done, f32[16,256]{1,0:T(8,128)S(1)} %mul.354, f32[512]{0:T(512)S(1)} %add_rsqrt_fusion), kind=kLoop, calls=%fused_computation.20 | loop fusion | flops 8388608 | bytes 8407040 | tf_op jit(solution)/shard_map/convert_element_type | solution.py:31
  120.9 6.1 %fusion.46 = f32[512,512]{1,0:T(8,128)S(1)} fusion(bf16[512,4096]{0,1:T(8,128)(2,1)S(1)} %bitcast.62, bf16[3,4096,512]{2,1,0:T(8,128)(2,1)} %param.10), kind=kOutput, calls=%fused_computation.40 | convolution fusion | flops 2148007936 | bytes 9437184 | tf_op jit(solution)/shard_map/dot_general | solution.py:34
  127.0 4.5 %fusion.40 = bf16[512,512]{1,0:T(8,128)(2,1)S(1)} fusion(f32[512,512]{1,0:T(8,128)S(1)} %fusion.46, bf16[512,4096]{0,1:T(8,128)(2,1)S(1)} %bitcast.63, bf16[3,4096,512]{2,1,0:T(8,128)(2,1)} %param.10), kind=kOutput, calls=%fused_computation.38 | convolution fusion | flops 2148532224 | bytes 9961472 | tf_op jit(solution)/shard_map/dot_general | solution.py:33
  131.6 3.1 %collective-permute-start = (bf16[127,512]{1,0:T(8,128)(2,1)S(1)}, bf16[127,512]{1,0:T(8,128)(2,1)S(1)}, u32[]{:S(2)}, u32[]{:S(2)}) collective-permute-start(bf16[127,512]{1,0:T(8,128)(2,1)S(1)} %slice.16), channel_id=1, source_target_pairs={{0,16},{16,32},{32,48},{48,64},{64,80},{80,96},{96,112},{112,128},... | collective-permute-start | bytes 390152 | tf_op jit(solution)/shard_map/ppermute | solution.py:24
  134.7 2.5 collective-permute-done
  137.2 0.1 pad_maximum_fusion
  137.4 39.9 %while.17 = (s32[]{:T(128)}, f32[512,512]{1,0:T(8,128)S(1)}, bf16[639,512]{1,0:T(8,128)(2,1)S(1)}, f32[128,512]{1,0:T(8,128)}, s32[]{:T(128)}, /*index=5*/s32[]{...) while((s32[]{:T(128)}, f32[512,512]{1,0:T(8,128)S(1)}, ...), condition=%wide.region_2.0_spmd.clone, body=%wide.region_1.0_spmd.clone.sunk | while | flops 6553667 | bytes 6341631 | solution.py:51
  137.4 1.0 constant_dynamic-slice_fusion.9
  138.5 1.4 fusion.57
  139.9 1.0 constant_dynamic-slice_fusion.9
  141.0 1.3 fusion.57
  142.4 1.0 constant_dynamic-slice_fusion.9
  143.5 1.4 fusion.57
  144.9 1.0 constant_dynamic-slice_fusion.9
  146.0 1.3 fusion.57
  147.4 1.0 constant_dynamic-slice_fusion.9
  148.5 1.4 fusion.57
  149.9 1.0 constant_dynamic-slice_fusion.9
  151.0 1.3 fusion.57
  152.4 1.0 constant_dynamic-slice_fusion.9
  153.5 1.4 fusion.57
  154.9 1.0 constant_dynamic-slice_fusion.9
  156.0 1.3 fusion.57
  157.4 1.0 constant_dynamic-slice_fusion.9
  158.4 1.4 fusion.57
  159.9 1.0 constant_dynamic-slice_fusion.9
  160.9 1.3 fusion.57
  162.4 1.0 constant_dynamic-slice_fusion.9
  163.4 1.4 fusion.57
  164.9 1.0 constant_dynamic-slice_fusion.9
  165.9 1.3 fusion.57
  167.4 1.0 constant_dynamic-slice_fusion.9
  168.4 1.4 fusion.57
  169.9 1.0 constant_dynamic-slice_fusion.9
  170.9 1.3 fusion.57
  172.4 1.0 constant_dynamic-slice_fusion.9
  173.4 1.4 fusion.57
  174.9 1.0 constant_dynamic-slice_fusion.9
  175.9 1.3 fusion.57
  177.3 11.2 %convolution_convert_fusion = bf16[512,4096]{1,0:T(8,128)(2,1)} fusion(bf16[512,4096]{1,0:T(8,128)(2,1)} %param.13, bf16[512,4096]{0,1:T(8,128)(2,1)} %bitcast.64, bf16[3,4096,512]{2,1,0:T(8,128)(2,1)} %param.10, f32[512,512]{1,0:T(8,128)S(1)} %get-tuple-element.156, bf16[512,512]{1,0:T(8,128)(2,1)S(1)} %fusion.40, f32[512]{0:T(512)S(1)} %copy-done.2), kind=kOutput, calls=%fused_computation.21 | convolution fusion | flops 4298899456 | bytes 18352128 | tf_op jit(solution)/shard_map/dot_general | solution.py:54
  188.5 0.0 reduce-scatter.2.cloned.1.call-update
  188.5 77.6 %reduce-scatter.2.cloned.1.call-done = bf16[512,256]{1,0:T(8,128)(2,1)} async-done(((bf16[512,4096]{1,0:T(8,128)(2,1)}), bf16[512,256]{1,0:T(8,128)(2,1)}) %reduce-scatter.2.cloned.1.call-update) | async-done | bytes 262160 | tf_op jit(solution)/shard_map/reduce_scatter | solution.py:55
  (10 shorter events, 0.1 us)
Async XLA Ops:
  10.0 12.0 %copy-start.1 = (f32[4096]{0:T(1024)S(1)}, f32[4096]{0:T(1024)}, u32[]{:S(2)}) copy-start(f32[4096]{0:T(1024)} %param.9) | copy-start | bytes 49156
  10.0 104.9 %all-to-all-start = ((bf16[16,512,256]{1,2,0:T(8,128)(2,1)}), bf16[16,512,256]{1,2,0:T(8,128)(2,1)}, u32[]{:S(2)}, u32[]{:S(2)}) async-start(bf16[16,512,256]{1,2,0:T(8,128)(2,1)} %stack.2), calls=%async_computation | async-start | bytes 8388608 | tf_op jit(solution)/shard_map/all_to_all | solution.py:11
  22.0 244.1 %reduce-scatter.2.cloned.1.call-start = ((), (), s32[]{:S(2)}) async-start(), calls=%async_computation.2 | async-start | bytes 4456448 | tf_op jit(solution)/shard_map/reduce_scatter | solution.py:55
  120.9 6.1 %copy-start = (bf16[16,512,256]{1,2,0:T(8,128)(2,1)}, bf16[16,512,256]{1,2,0:T(8,128)(2,1)S(1)}, u32[]{:S(2)}) copy-start(bf16[16,512,256]{1,2,0:T(8,128)(2,1)S(1)} %fusion.9) | copy-start | bytes 12582916
  131.6 5.7 %collective-permute-start = (bf16[127,512]{1,0:T(8,128)(2,1)S(1)}, bf16[127,512]{1,0:T(8,128)(2,1)S(1)}, u32[]{:S(2)}, u32[]{:S(2)}) collective-permute-start(bf16[127,512]{1,0:T(8,128)(2,1)S(1)} %slice.16), channel_id=1, source_target_pairs={{0,16},{16,32},{32,48},{48,64},{64,80},{80,96},{96,112},{112,128},... | collective-permute-start | bytes 390152 | tf_op jit(solution)/shard_map/ppermute | solution.py:24
  137.3 39.9 %copy-start.2 = (f32[512]{0:T(512)S(1)}, f32[512]{0:T(512)}, u32[]{:S(2)}) copy-start(f32[512]{0:T(512)} %param.12) | copy-start | bytes 6148
Sparse Core Ops, SparseCore 0:
  188.6 77.4 reduce-scatter.1
